TPU v7x, 512 devices: a whole 4x4x16 slice. The times are simulated.
512 devices in a mesh: leaf: 32 (over z, core), front: 16 (over y, x).
Axes of the slice: x: 4, y: 4, z: 16, core: 2. Of those that a mesh axis runs over, the one named last changes fastest.
Arguments:
- forcing: bfloat16 [32, 10240, 128], P('leaf', 'front'), may hold values from -6 to 6
- live: int32 [2, 32], replicated, may hold values from 40 to 80, as said below
- lower_inv: bfloat16 [32, 10240, 960], P('leaf', 'front'), may hold values from -0.0625 to 0.0625
- lower_upd: bfloat16 [32, 10240, 640], P('leaf', 'front'), may hold values from -0.0625 to 0.0625
- upper_inv: bfloat16 [32, 10240, 960], P('leaf', 'front'), may hold values from -0.0625 to 0.0625
- upper_upd: bfloat16 [32, 10240, 640], P('leaf', 'front'), may hold values from -0.0625 to 0.0625
Outputs:
- solution: bfloat16 [2, 32, 10240, 128], P(None, 'leaf', 'front')
Inputs may be any that keep to these rules, and one draw needn't show every extreme that they name: Entries (l, j) with j at or beyond 2**(1 - l) are not read. The root's separator is live in full.
All inputs are finite; a program needn't handle non-finite values.
Results may differ from a plain program's by a relative error of at most 0.008.
Values may be sent and summed in bfloat16 or wider, within the bound.
No kernel may reach another device: no remote copies, remote signals or barrier semaphores. Data moves between devices by JAX's collectives and lax.ppermute only.
A program may use at most 64 MiB of HBM per device.

v0:
```python
import jax
import jax.numpy as jnp
from jax import lax
from jax.sharding import PartitionSpec as P

BLK = 128
LEV = 2


def from_root(array, axis, root):
    mine = lax.axis_index(axis) == root
    return lax.psum(jnp.where(mine, array, jnp.zeros_like(array)), axis)


def partner(block, axis, bit):
    count = lax.axis_size(axis)
    route = []
    for low in range(count):
        high = low | 1 << bit
        if high != low and high < count:
            route += [(low, high), (high, low)]
    return lax.ppermute(block, axis, route)


def body(forcing, live, lower_inv, lower_upd, upper_inv, upper_upd):
    n_leaf = lax.axis_size("leaf")
    sep_dev = forcing.shape[1]
    n_rhs = forcing.shape[2]
    sep = sep_dev * lax.axis_size("front")
    skip = n_leaf.bit_length() - LEV
    leaf_id = lax.axis_index("leaf")
    front_id = lax.axis_index("front")
    rows = front_id * sep_dev + jnp.arange(sep_dev)
    first = 2 * (sep >> skip)

    def level_mask(level):
        count = live[level][leaf_id >> level + skip]
        return (rows < count * BLK).astype(jnp.float32)[:, None]

    def fetch(block, level, residual_kind):
        depth = level + skip
        width = sep >> depth
        start = (leaf_id & (1 << depth) - 1) * width
        owner = start // sep_dev
        if residual_kind:
            piece = from_root(block, "front", owner)
        else:
            piece = from_root(block, "front", owner)
        return lax.dynamic_slice_in_dim(piece, start % sep_dev, width, 0)

    def subtree_total(partial_value, depth):
        for bit in range(depth):
            partial_value = partial_value + partner(partial_value, "leaf", bit)
        return partial_value

    residual = subtree_total(forcing[0].astype(jnp.float32), skip)
    forward = []
    for level in range(LEV):
        depth = level + skip
        width = sep >> depth
        offset = first - 2 * width
        mask = level_mask(level)
        masked = (mask * residual).astype(jnp.bfloat16)
        picked = fetch(masked, level, True)
        y_term = jnp.dot(
            lower_inv[0, :, offset : offset + width], picked, preferred_element_type=jnp.float32
        )
        if level < LEV - 1:
            c_term = jnp.dot(
                lower_upd[0, :, offset : offset + width], picked, preferred_element_type=jnp.float32
            )
            summed = subtree_total(jnp.concatenate([y_term, -c_term], 0), depth)
            y_sum = summed[:sep_dev]
            loads = summed[sep_dev:]
            residual = loads + partner(loads, "leaf", depth)
        else:
            y_sum = subtree_total(y_term, depth)
        forward.append((mask * y_sum).astype(jnp.bfloat16))
    results = [None] * LEV
    above = None
    for level in reversed(range(LEV)):
        depth = level + skip
        width = sep >> depth
        offset = first - 2 * width
        mask = level_mask(level)
        if above is None:
            picked = fetch(forward[level], level, False)
            term = jnp.dot(
                upper_inv[0, :, offset : offset + width], picked, preferred_element_type=jnp.float32
            )
        else:
            picked = fetch(jnp.concatenate([forward[level], above], 1), level, False)
            term = jnp.dot(
                upper_inv[0, :, offset : offset + width],
                picked[:, :n_rhs],
                preferred_element_type=jnp.float32,
            )
            term = term - jnp.dot(
                upper_upd[0, :, offset : offset + width],
                picked[:, n_rhs:],
                preferred_element_type=jnp.float32,
            )
        solved = (mask * subtree_total(term, depth)).astype(jnp.bfloat16)
        results[level] = solved
        above = solved
    return jnp.stack(results)[:, None]


def solution(mesh):
    return jax.shard_map(
        body,
        mesh=mesh,
        in_specs=(
            P("leaf", "front", None),
            P(),
            P("leaf", "front", None),
            P("leaf", "front", None),
            P("leaf", "front", None),
            P("leaf", "front", None),
        ),
        out_specs=P(None, "leaf", "front", None),
        check_vma=False,
    )
```

profile of v0, /device:TPU:1, one launch (start us, length us, event | category | flops | bytes accessed | tf_op | source)
XLA Modules:
  0.0 972.4 jit_solution(18222243295650057958)
XLA Ops:
  7.7 8.8 collective-permute-start
  19.7 8.9 collective-permute-done.1
  30.7 17.4 %collective-permute-done.2 = f32[640,128]{0,1:T(8,128)S(1)} collective-permute-done((f32[640,128]{0,1:T(8,128)S(1)}, f32[640,128]{0,1:T(8,128)S(1)}, u32[]{:S(2)}, u32[]{:S(2)}) %collective-permute-start.2) | collective-permute-done | bytes 327712 | tf_op jit(solution)/shard_map/ppermute | solution.py:22
  53.1 29.1 %collective-permute-done.3 = f32[640,128]{0,1:T(8,128)S(1)} collective-permute-done((f32[640,128]{0,1:T(8,128)S(1)}, f32[640,128]{0,1:T(8,128)S(1)}, u32[]{:S(2)}, u32[]{:S(2)}) %collective-permute-start.3) | collective-permute-done | bytes 327712 | tf_op jit(solution)/shard_map/ppermute | solution.py:22
  82.9 112.0 %all-reduce.5.cloned.1.call-done = bf16[640,128]{0,1:T(8,128)(2,1)} async-done(((bf16[640,128]{0,1:T(8,128)(2,1)}), bf16[640,128]{0,1:T(8,128)(2,1)}) %all-reduce.5.cloned.1.call-update) | async-done | bytes 163856 | tf_op jit(solution)/shard_map/psum | solution.py:12
  206.1 14.7 %collective-permute-done.5 = f32[1280,128]{0,1:T(8,128)S(1)} collective-permute-done((f32[1280,128]{0,1:T(8,128)S(1)}, f32[1280,128]{0,1:T(8,128)S(1)}, u32[]{:S(2)}, u32[]{:S(2)}) %collective-permute-start.5) | collective-permute-done | bytes 655392 | tf_op jit(solution)/shard_map/ppermute | solution.py:22
  225.0 28.3 %collective-permute-done.6 = f32[1280,128]{0,1:T(8,128)S(1)} collective-permute-done((f32[1280,128]{0,1:T(8,128)S(1)}, f32[1280,128]{0,1:T(8,128)S(1)}, u32[]{:S(2)}, u32[]{:S(2)}) %collective-permute-start.6) | collective-permute-done | bytes 655392 | tf_op jit(solution)/shard_map/ppermute | solution.py:22
  253.3 7.4 collective-permute-start.7
  260.7 63.4 %collective-permute-done.7 = f32[1280,128]{0,1:T(8,128)S(1)} collective-permute-done((f32[1280,128]{0,1:T(8,128)S(1)}, f32[1280,128]{0,1:T(8,128)S(1)}, u32[]{:S(2)}, u32[]{:S(2)}) %collective-permute-start.7) | collective-permute-done | bytes 655392 | tf_op jit(solution)/shard_map/ppermute | solution.py:22
  324.2 11.1 %collective-permute-start.8 = (f32[640,128]{0,1:T(8,128)S(1)}, f32[640,128]{0,1:T(8,128)S(1)}, u32[]{:S(2)}, u32[]{:S(2)}) collective-permute-start(f32[640,128]{0,1:T(8,128)S(1)} %get-tuple-element.6), channel_id=1, source_target_pairs={{0,256},{256,0},{16,272},{272,16},{32,288},{288,32},{48,304},{304,... | collective-permute-start | bytes 983048 | tf_op jit(solution)/shard_map/ppermute | solution.py:22
  336.0 12.4 %collective-permute-done.8 = f32[640,128]{0,1:T(8,128)S(1)} collective-permute-done((f32[640,128]{0,1:T(8,128)S(1)}, f32[640,128]{0,1:T(8,128)S(1)}, u32[]{:S(2)}, u32[]{:S(2)}) %collective-permute-start.8) | collective-permute-done | bytes 327712 | tf_op jit(solution)/shard_map/ppermute | solution.py:22
  349.2 113.3 %all-reduce.7.cloned.1.call-done = bf16[640,128]{0,1:T(8,128)(2,1)} async-done(((bf16[640,128]{0,1:T(8,128)(2,1)}), bf16[640,128]{0,1:T(8,128)(2,1)}) %all-reduce.7.cloned.1.call-update) | async-done | bytes 163856 | tf_op jit(solution)/shard_map/psum | solution.py:12
  463.7 4.4 collective-permute-start.9
  472.6 7.6 collective-permute-done.10
  484.5 14.2 %collective-permute-done.11 = f32[640,128]{0,1:T(8,128)S(1)} collective-permute-done((f32[640,128]{0,1:T(8,128)S(1)}, f32[640,128]{0,1:T(8,128)S(1)}, u32[]{:S(2)}, u32[]{:S(2)}) %collective-permute-start.11) | collective-permute-done | bytes 327712 | tf_op jit(solution)/shard_map/ppermute | solution.py:22
  498.7 7.5 collective-permute-start.12
  506.2 28.2 %collective-permute-done.12 = f32[640,128]{0,1:T(8,128)S(1)} collective-permute-done((f32[640,128]{0,1:T(8,128)S(1)}, f32[640,128]{0,1:T(8,128)S(1)}, u32[]{:S(2)}, u32[]{:S(2)}) %collective-permute-start.12) | collective-permute-done | bytes 327712 | tf_op jit(solution)/shard_map/ppermute | solution.py:22
  534.5 18.2 %collective-permute-start.13 = (f32[640,128]{0,1:T(8,128)S(1)}, f32[640,128]{0,1:T(8,128)S(1)}, u32[]{:S(2)}, u32[]{:S(2)}) collective-permute-start(f32[640,128]{0,1:T(8,128)S(1)} %add.131), channel_id=1, source_target_pairs={{0,256},{256,0},{16,272},{272,16},{32,288},{288,32},{48,304},{304,... | collective-permute-start | bytes 983048 | tf_op jit(solution)/shard_map/ppermute | solution.py:22
  552.7 14.1 %collective-permute-done.13 = f32[640,128]{0,1:T(8,128)S(1)} collective-permute-done((f32[640,128]{0,1:T(8,128)S(1)}, f32[640,128]{0,1:T(8,128)S(1)}, u32[]{:S(2)}, u32[]{:S(2)}) %collective-permute-start.13) | collective-permute-done | bytes 327712 | tf_op jit(solution)/shard_map/ppermute | solution.py:22
  567.6 110.0 %all-reduce.9.cloned.1.call-done = bf16[640,128]{0,1:T(8,128)(2,1)} async-done(((bf16[640,128]{0,1:T(8,128)(2,1)}), bf16[640,128]{0,1:T(8,128)(2,1)}) %all-reduce.9.cloned.1.call-update) | async-done | bytes 163856 | tf_op jit(solution)/shard_map/psum | solution.py:12
  678.8 4.4 collective-permute-start.14
  687.7 7.6 collective-permute-done.15
  699.5 14.2 %collective-permute-done.16 = f32[640,128]{0,1:T(8,128)S(1)} collective-permute-done((f32[640,128]{0,1:T(8,128)S(1)}, f32[640,128]{0,1:T(8,128)S(1)}, u32[]{:S(2)}, u32[]{:S(2)}) %collective-permute-start.16) | collective-permute-done | bytes 327712 | tf_op jit(solution)/shard_map/ppermute | solution.py:22
  713.7 7.4 collective-permute-start.17
  721.1 28.2 %collective-permute-done.17 = f32[640,128]{0,1:T(8,128)S(1)} collective-permute-done((f32[640,128]{0,1:T(8,128)S(1)}, f32[640,128]{0,1:T(8,128)S(1)}, u32[]{:S(2)}, u32[]{:S(2)}) %collective-permute-start.17) | collective-permute-done | bytes 327712 | tf_op jit(solution)/shard_map/ppermute | solution.py:22
  749.4 18.2 %collective-permute-start.18 = (f32[640,128]{0,1:T(8,128)S(1)}, f32[640,128]{0,1:T(8,128)S(1)}, u32[]{:S(2)}, u32[]{:S(2)}) collective-permute-start(f32[640,128]{0,1:T(8,128)S(1)} %add.136), channel_id=1, source_target_pairs={{0,256},{256,0},{16,272},{272,16},{32,288},{288,32},{48,304},{304,... | collective-permute-start | bytes 983048 | tf_op jit(solution)/shard_map/ppermute | solution.py:22
  767.6 14.1 %collective-permute-done.18 = f32[640,128]{0,1:T(8,128)S(1)} collective-permute-done((f32[640,128]{0,1:T(8,128)S(1)}, f32[640,128]{0,1:T(8,128)S(1)}, u32[]{:S(2)}, u32[]{:S(2)}) %collective-permute-start.18) | collective-permute-done | bytes 327712 | tf_op jit(solution)/shard_map/ppermute | solution.py:22
  782.6 110.6 %all-reduce.11.cloned.1.call-done = bf16[640,256]{0,1:T(8,128)(2,1)} async-done(((bf16[640,256]{0,1:T(8,128)(2,1)}), bf16[640,256]{0,1:T(8,128)(2,1)}) %all-reduce.11.cloned.1.call-update) | async-done | bytes 327696 | tf_op jit(solution)/shard_map/psum | solution.py:12
  903.2 7.6 collective-permute-done.20
  915.1 14.2 %collective-permute-done.21 = f32[640,128]{0,1:T(8,128)S(1)} collective-permute-done((f32[640,128]{0,1:T(8,128)S(1)}, f32[640,128]{0,1:T(8,128)S(1)}, u32[]{:S(2)}, u32[]{:S(2)}) %collective-permute-start.21) | collective-permute-done | bytes 327712 | tf_op jit(solution)/shard_map/ppermute | solution.py:22
  929.3 7.4 collective-permute-start.22
  936.7 28.2 %collective-permute-done.22 = f32[640,128]{0,1:T(8,128)S(1)} collective-permute-done((f32[640,128]{0,1:T(8,128)S(1)}, f32[640,128]{0,1:T(8,128)S(1)}, u32[]{:S(2)}, u32[]{:S(2)}) %collective-permute-start.22) | collective-permute-done | bytes 327712 | tf_op jit(solution)/shard_map/ppermute | solution.py:22
  (80 shorter events, 65.6 us)
Async XLA Ops:
  6.5 189.7 %copy-start = (bf16[1,640,640]{2,1,0:T(8,128)(2,1)S(1)}, bf16[1,640,640]{2,1,0:T(8,128)(2,1)}, u32[]{:S(2)}) copy-start(bf16[1,640,640]{2,1,0:T(8,128)(2,1)} %param.9) | copy-start | bytes 2457604
  6.5 188.4 %all-reduce.5.cloned.1.call-start = ((), (), s32[]{:S(2)}) async-start(), calls=%async_computation | async-start | bytes 327680 | tf_op jit(solution)/shard_map/psum | solution.py:12
  7.7 44.0 %copy-start.6 = (s32[2,32]{1,0:T(2,128)S(1)}, s32[2,32]{1,0:T(2,128)}, u32[]{:S(2)}) copy-start(s32[2,32]{1,0:T(2,128)} %param.7) | copy-start | bytes 772
  7.7 10.0 %collective-permute-start = (f32[640,128]{0,1:T(8,128)S(1)}, f32[640,128]{0,1:T(8,128)S(1)}, u32[]{:S(2)}, u32[]{:S(2)}) collective-permute-start(f32[640,128]{0,1:T(8,128)S(1)} %bitcast_convert_fusion), channel_id=1, source_target_pairs={{0,16},{16,0},{32,48},{48,32},{64,80},{80,64},{96,112},{112,96},{1... | collective-permute-start | bytes 983048 | tf_op jit(solution)/shard_map/ppermute | solution.py:22
  17.8 10.8 %collective-permute-start.1 = (f32[640,128]{0,1:T(8,128)S(1)}, f32[640,128]{0,1:T(8,128)S(1)}, u32[]{:S(2)}, u32[]{:S(2)}) collective-permute-start(f32[640,128]{0,1:T(8,128)S(1)} %fusion.22), channel_id=1, source_target_pairs={{0,32},{32,0},{16,48},{48,16},{64,96},{96,64},{80,112},{112,80},{1... | collective-permute-start | bytes 983048 | tf_op jit(solution)/shard_map/ppermute | solution.py:22
  28.6 166.3 %copy-start.1 = (bf16[1,640,960]{1,2,0:T(8,128)(2,1)S(1)}, bf16[1,640,960]{1,2,0:T(8,128)(2,1)}, u32[]{:S(2)}) copy-start(bf16[1,640,960]{1,2,0:T(8,128)(2,1)} %param.8) | copy-start | bytes 3686404
  28.7 19.5 %collective-permute-start.2 = (f32[640,128]{0,1:T(8,128)S(1)}, f32[640,128]{0,1:T(8,128)S(1)}, u32[]{:S(2)}, u32[]{:S(2)}) collective-permute-start(f32[640,128]{0,1:T(8,128)S(1)} %add.117), channel_id=1, source_target_pairs={{0,64},{64,0},{16,80},{80,16},{32,96},{96,32},{48,112},{112,48},{1... | collective-permute-start | bytes 983048 | tf_op jit(solution)/shard_map/ppermute | solution.py:22
  48.2 33.9 %collective-permute-start.3 = (f32[640,128]{0,1:T(8,128)S(1)}, f32[640,128]{0,1:T(8,128)S(1)}, u32[]{:S(2)}, u32[]{:S(2)}) collective-permute-start(f32[640,128]{0,1:T(8,128)S(1)} %add.118), channel_id=1, source_target_pairs={{0,128},{128,0},{16,144},{144,16},{32,160},{160,32},{48,176},{176,... | collective-permute-start | bytes 983048 | tf_op jit(solution)/shard_map/ppermute | solution.py:22
  82.9 379.7 %all-reduce.7.cloned.1.call-start = ((), (), s32[]{:S(2)}) async-start(), calls=%async_computation.1 | async-start | bytes 327680 | tf_op jit(solution)/shard_map/psum | solution.py:12
  196.7 6.1 collective-permute-start.4
  202.9 17.8 %collective-permute-start.5 = (f32[1280,128]{0,1:T(8,128)S(1)}, f32[1280,128]{0,1:T(8,128)S(1)}, u32[]{:S(2)}, u32[]{:S(2)}) collective-permute-start(f32[1280,128]{0,1:T(8,128)S(1)} %fusion.29), channel_id=1, source_target_pairs={{0,32},{32,0},{16,48},{48,16},{64,96},{96,64},{80,112},{112,80},{1... | collective-permute-start | bytes 1966088 | tf_op jit(solution)/shard_map/ppermute | solution.py:22
  220.8 32.4 %collective-permute-start.6 = (f32[1280,128]{0,1:T(8,128)S(1)}, f32[1280,128]{0,1:T(8,128)S(1)}, u32[]{:S(2)}, u32[]{:S(2)}) collective-permute-start(f32[1280,128]{0,1:T(8,128)S(1)} %add.121), channel_id=1, source_target_pairs={{0,64},{64,0},{16,80},{80,16},{32,96},{96,32},{48,112},{112,48},{1... | collective-permute-start | bytes 1966088 | tf_op jit(solution)/shard_map/ppermute | solution.py:22
  253.3 70.8 %collective-permute-start.7 = (f32[1280,128]{0,1:T(8,128)S(1)}, f32[1280,128]{0,1:T(8,128)S(1)}, u32[]{:S(2)}, u32[]{:S(2)}) collective-permute-start(f32[1280,128]{0,1:T(8,128)S(1)} %add.122), channel_id=1, source_target_pairs={{0,128},{128,0},{16,144},{144,16},{32,160},{160,32},{48,176},{176,... | collective-permute-start | bytes 1966088 | tf_op jit(solution)/shard_map/ppermute | solution.py:22
  324.2 24.2 %collective-permute-start.8 = (f32[640,128]{0,1:T(8,128)S(1)}, f32[640,128]{0,1:T(8,128)S(1)}, u32[]{:S(2)}, u32[]{:S(2)}) collective-permute-start(f32[640,128]{0,1:T(8,128)S(1)} %get-tuple-element.6), channel_id=1, source_target_pairs={{0,256},{256,0},{16,272},{272,16},{32,288},{288,32},{48,304},{304,... | collective-permute-start | bytes 983048 | tf_op jit(solution)/shard_map/ppermute | solution.py:22
  349.1 328.4 %all-reduce.9.cloned.1.call-start = ((), (), s32[]{:S(2)}) async-start(), calls=%async_computation.2 | async-start | bytes 327680 | tf_op jit(solution)/shard_map/psum | solution.py:12
  463.7 5.7 collective-permute-start.9
  469.4 10.8 %collective-permute-start.10 = (f32[640,128]{0,1:T(8,128)S(1)}, f32[640,128]{0,1:T(8,128)S(1)}, u32[]{:S(2)}, u32[]{:S(2)}) collective-permute-start(f32[640,128]{0,1:T(8,128)S(1)} %add.128), channel_id=1, source_target_pairs={{0,32},{32,0},{16,48},{48,16},{64,96},{96,64},{80,112},{112,80},{1... | collective-permute-start | bytes 983048 | tf_op jit(solution)/shard_map/ppermute | solution.py:22
  480.3 18.4 %collective-permute-start.11 = (f32[640,128]{0,1:T(8,128)S(1)}, f32[640,128]{0,1:T(8,128)S(1)}, u32[]{:S(2)}, u32[]{:S(2)}) collective-permute-start(f32[640,128]{0,1:T(8,128)S(1)} %add.129), channel_id=1, source_target_pairs={{0,64},{64,0},{16,80},{80,16},{32,96},{96,32},{48,112},{112,48},{1... | collective-permute-start | bytes 983048 | tf_op jit(solution)/shard_map/ppermute | solution.py:22
  498.7 178.9 %copy-start.2 = (bf16[1,640,960]{1,2,0:T(8,128)(2,1)S(1)}, bf16[1,640,960]{1,2,0:T(8,128)(2,1)}, u32[]{:S(2)}) copy-start(bf16[1,640,960]{1,2,0:T(8,128)(2,1)} %param.10) | copy-start | bytes 3686404
  498.7 35.7 %collective-permute-start.12 = (f32[640,128]{0,1:T(8,128)S(1)}, f32[640,128]{0,1:T(8,128)S(1)}, u32[]{:S(2)}, u32[]{:S(2)}) collective-permute-start(f32[640,128]{0,1:T(8,128)S(1)} %add.130), channel_id=1, source_target_pairs={{0,128},{128,0},{16,144},{144,16},{32,160},{160,32},{48,176},{176,... | collective-permute-start | bytes 983048 | tf_op jit(solution)/shard_map/ppermute | solution.py:22
  534.5 32.3 %collective-permute-start.13 = (f32[640,128]{0,1:T(8,128)S(1)}, f32[640,128]{0,1:T(8,128)S(1)}, u32[]{:S(2)}, u32[]{:S(2)}) collective-permute-start(f32[640,128]{0,1:T(8,128)S(1)} %add.131), channel_id=1, source_target_pairs={{0,256},{256,0},{16,272},{272,16},{32,288},{288,32},{48,304},{304,... | collective-permute-start | bytes 983048 | tf_op jit(solution)/shard_map/ppermute | solution.py:22
  567.5 325.7 %all-reduce.11.cloned.1.call-start = ((), (), s32[]{:S(2)}) async-start(), calls=%async_computation.3 | async-start | bytes 655360 | tf_op jit(solution)/shard_map/psum | solution.py:12
  678.8 5.7 collective-permute-start.14
  684.5 10.8 %collective-permute-start.15 = (f32[640,128]{0,1:T(8,128)S(1)}, f32[640,128]{0,1:T(8,128)S(1)}, u32[]{:S(2)}, u32[]{:S(2)}) collective-permute-start(f32[640,128]{0,1:T(8,128)S(1)} %add.133), channel_id=1, source_target_pairs={{0,32},{32,0},{16,48},{48,16},{64,96},{96,64},{80,112},{112,80},{1... | collective-permute-start | bytes 983048 | tf_op jit(solution)/shard_map/ppermute | solution.py:22
  695.3 18.4 %collective-permute-start.16 = (f32[640,128]{0,1:T(8,128)S(1)}, f32[640,128]{0,1:T(8,128)S(1)}, u32[]{:S(2)}, u32[]{:S(2)}) collective-permute-start(f32[640,128]{0,1:T(8,128)S(1)} %add.134), channel_id=1, source_target_pairs={{0,64},{64,0},{16,80},{80,16},{32,96},{96,32},{48,112},{112,48},{1... | collective-permute-start | bytes 983048 | tf_op jit(solution)/shard_map/ppermute | solution.py:22
  713.7 35.6 %collective-permute-start.17 = (f32[640,128]{0,1:T(8,128)S(1)}, f32[640,128]{0,1:T(8,128)S(1)}, u32[]{:S(2)}, u32[]{:S(2)}) collective-permute-start(f32[640,128]{0,1:T(8,128)S(1)} %add.135), channel_id=1, source_target_pairs={{0,128},{128,0},{16,144},{144,16},{32,160},{160,32},{48,176},{176,... | collective-permute-start | bytes 983048 | tf_op jit(solution)/shard_map/ppermute | solution.py:22
  749.4 32.3 %collective-permute-start.18 = (f32[640,128]{0,1:T(8,128)S(1)}, f32[640,128]{0,1:T(8,128)S(1)}, u32[]{:S(2)}, u32[]{:S(2)}) collective-permute-start(f32[640,128]{0,1:T(8,128)S(1)} %add.136), channel_id=1, source_target_pairs={{0,256},{256,0},{16,272},{272,16},{32,288},{288,32},{48,304},{304,... | collective-permute-start | bytes 983048 | tf_op jit(solution)/shard_map/ppermute | solution.py:22
  781.7 112.8 %copy-start.3 = (bf16[1,640,640]{2,1,0:T(8,128)(2,1)S(1)}, bf16[1,640,640]{2,1,0:T(8,128)(2,1)}, u32[]{:S(2)}) copy-start(bf16[1,640,640]{2,1,0:T(8,128)(2,1)} %param.11) | copy-start | bytes 2457604
  894.9 5.1 collective-permute-start.19
  900.1 10.8 %collective-permute-start.20 = (f32[640,128]{0,1:T(8,128)S(1)}, f32[640,128]{0,1:T(8,128)S(1)}, u32[]{:S(2)}, u32[]{:S(2)}) collective-permute-start(f32[640,128]{0,1:T(8,128)S(1)} %add.138), channel_id=1, source_target_pairs={{0,32},{32,0},{16,48},{48,16},{64,96},{96,64},{80,112},{112,80},{1... | collective-permute-start | bytes 983048 | tf_op jit(solution)/shard_map/ppermute | solution.py:22
  910.9 18.4 %collective-permute-start.21 = (f32[640,128]{0,1:T(8,128)S(1)}, f32[640,128]{0,1:T(8,128)S(1)}, u32[]{:S(2)}, u32[]{:S(2)}) collective-permute-start(f32[640,128]{0,1:T(8,128)S(1)} %add.139), channel_id=1, source_target_pairs={{0,64},{64,0},{16,80},{80,16},{32,96},{96,32},{48,112},{112,48},{1... | collective-permute-start | bytes 983048 | tf_op jit(solution)/shard_map/ppermute | solution.py:22
  929.3 35.6 %collective-permute-start.22 = (f32[640,128]{0,1:T(8,128)S(1)}, f32[640,128]{0,1:T(8,128)S(1)}, u32[]{:S(2)}, u32[]{:S(2)}) collective-permute-start(f32[640,128]{0,1:T(8,128)S(1)} %add.140), channel_id=1, source_target_pairs={{0,128},{128,0},{16,144},{144,16},{32,160},{160,32},{48,176},{176,... | collective-permute-start | bytes 983048 | tf_op jit(solution)/shard_map/ppermute | solution.py:22
  (2 other events, 2.6 us)
Sparse Core Ops, SparseCore 0:
  83.0 111.9 all-reduce.4
  349.3 113.2 all-reduce.6
  567.7 109.8 all-reduce.8
  782.7 110.4 all-reduce.10
where the time goes:
time: 973 us; the launch traced here: 972 us
  waiting for transfers between devices  805 us (83%)
  starting transfers between devices  140 us (14%)
  between operations  13.6 us (1%)
    psum x4, waiting for transfers between devices, from_root(): return lax.psum(jnp.where(mine, array, jnp.zeros_like(array)), axis)  446 us
    ppermute x23, waiting for transfers between devices, partner(): return lax.ppermute(block, axis, route)  359 us
    ppermute x23, starting transfers between devices, partner(): return lax.ppermute(block, axis, route)  140 us
  transfers between devices with their start and end apart: 27, of which 27 were waited for; matrix products, arithmetic and copies ran while one was open for 0% of the time, Pallas kernels for 0%

commit v1 on v0

--- a/solution.py
+++ b/solution.py
@@ -9,7 +9,7 @@
 
 def from_root(array, axis, root):
     mine = lax.axis_index(axis) == root
-    return lax.psum(jnp.where(mine, array, jnp.zeros_like(array)), axis)
+    return jnp.sum(lax.all_gather(jnp.where(mine, array, jnp.zeros_like(array)), axis), axis=0)
 
 
 def partner(block, axis, bit):

time: 973 us -> 786 us (0.81)
  waiting for transfers between devices: 805 us -> 610 us
    psum x4 -> x0, waiting for transfers between devices: 446 us -> none  [from_root(): return lax.psum(jnp.where(mine, array, jnp.zeros_like(array)), axis)]
    all_gather x0 -> x4, waiting for transfers between devices: none -> 251 us  [from_root(): lax.all_gather(jnp.where(mine, array, jnp.zeros_like(array)), axis)]
where the time goes in v1:
time: 786 us; the launch traced here: 785 us
  waiting for transfers between devices  610 us (78%)
  starting transfers between devices  138 us (18%)
  between operations  13.7 us (2%)
  other arithmetic  12.2 us (2%)
  local copies, waits for them, and re-layouts  9.65 us (1%)
    ppermute x23, waiting for transfers between devices, partner(): return lax.ppermute(block, axis, route)  359 us
    all_gather x4, waiting for transfers between devices, from_root(): lax.all_gather(jnp.where(mine, array, jnp.zeros_like(array)), axis)  251 us
    ppermute x23, starting transfers between devices, partner(): return lax.ppermute(block, axis, route)  137 us
  transfers between devices with their start and end apart: 27, of which 27 were waited for; matrix products, arithmetic and copies ran while one was open for 0% of the time, Pallas kernels for 0%

profile of v1, /device:TPU:1, one launch (start us, length us, event | category | flops | bytes accessed | tf_op | source)
XLA Modules:
  0.0 784.9 jit_solution(10403242534536177562)
XLA Ops:
  7.7 8.8 %collective-permute-start = (f32[640,128]{0,1:T(8,128)S(1)}, f32[640,128]{0,1:T(8,128)S(1)}, u32[]{:S(2)}, u32[]{:S(2)}) collective-permute-start(f32[640,128]{0,1:T(8,128)S(1)} %bitcast_convert_fusion), channel_id=1, source_target_pairs={{0,16},{16,0},{32,48},{48,32},{64,80},{80,64},{96,112},{112,96},{1... | collective-permute-start | bytes 983048 | tf_op jit(solution)/shard_map/ppermute | solution.py:22
  19.7 8.9 %collective-permute-done.1 = f32[640,128]{0,1:T(8,128)S(1)} collective-permute-done((f32[640,128]{0,1:T(8,128)S(1)}, f32[640,128]{0,1:T(8,128)S(1)}, u32[]{:S(2)}, u32[]{:S(2)}) %collective-permute-start.1) | collective-permute-done | bytes 327712 | tf_op jit(solution)/shard_map/ppermute | solution.py:22
  30.6 17.4 %collective-permute-done.2 = f32[640,128]{0,1:T(8,128)S(1)} collective-permute-done((f32[640,128]{0,1:T(8,128)S(1)}, f32[640,128]{0,1:T(8,128)S(1)}, u32[]{:S(2)}, u32[]{:S(2)}) %collective-permute-start.2) | collective-permute-done | bytes 327712 | tf_op jit(solution)/shard_map/ppermute | solution.py:22
  52.9 29.1 %collective-permute-done.3 = f32[640,128]{0,1:T(8,128)S(1)} collective-permute-done((f32[640,128]{0,1:T(8,128)S(1)}, f32[640,128]{0,1:T(8,128)S(1)}, u32[]{:S(2)}, u32[]{:S(2)}) %collective-permute-start.3) | collective-permute-done | bytes 327712 | tf_op jit(solution)/shard_map/ppermute | solution.py:22
  82.8 60.2 %all-gather.10.cloned.1.call-done = bf16[10240,128]{0,1:T(8,128)(2,1)} async-done(((bf16[640,128]{0,1:T(8,128)(2,1)}), bf16[10240,128]{0,1:T(8,128)(2,1)}) %all-gather.10.cloned.1.call-update) | async-done | bytes 2621456 | tf_op jit(solution)/shard_map/all_gather | solution.py:12
  156.3 14.7 %collective-permute-done.5 = f32[1280,128]{0,1:T(8,128)S(1)} collective-permute-done((f32[1280,128]{0,1:T(8,128)S(1)}, f32[1280,128]{0,1:T(8,128)S(1)}, u32[]{:S(2)}, u32[]{:S(2)}) %collective-permute-start.5) | collective-permute-done | bytes 655392 | tf_op jit(solution)/shard_map/ppermute | solution.py:22
  175.2 28.3 %collective-permute-done.6 = f32[1280,128]{0,1:T(8,128)S(1)} collective-permute-done((f32[1280,128]{0,1:T(8,128)S(1)}, f32[1280,128]{0,1:T(8,128)S(1)}, u32[]{:S(2)}, u32[]{:S(2)}) %collective-permute-start.6) | collective-permute-done | bytes 655392 | tf_op jit(solution)/shard_map/ppermute | solution.py:22
  203.5 7.4 collective-permute-start.7
  210.9 63.4 %collective-permute-done.7 = f32[1280,128]{0,1:T(8,128)S(1)} collective-permute-done((f32[1280,128]{0,1:T(8,128)S(1)}, f32[1280,128]{0,1:T(8,128)S(1)}, u32[]{:S(2)}, u32[]{:S(2)}) %collective-permute-start.7) | collective-permute-done | bytes 655392 | tf_op jit(solution)/shard_map/ppermute | solution.py:22
  274.4 11.1 %collective-permute-start.8 = (f32[640,128]{0,1:T(8,128)S(1)}, f32[640,128]{0,1:T(8,128)S(1)}, u32[]{:S(2)}, u32[]{:S(2)}) collective-permute-start(f32[640,128]{0,1:T(8,128)S(1)} %get-tuple-element.6), channel_id=1, source_target_pairs={{0,256},{256,0},{16,272},{272,16},{32,288},{288,32},{48,304},{304,... | collective-permute-start | bytes 983048 | tf_op jit(solution)/shard_map/ppermute | solution.py:22
  286.1 12.5 %collective-permute-done.8 = f32[640,128]{0,1:T(8,128)S(1)} collective-permute-done((f32[640,128]{0,1:T(8,128)S(1)}, f32[640,128]{0,1:T(8,128)S(1)}, u32[]{:S(2)}, u32[]{:S(2)}) %collective-permute-start.8) | collective-permute-done | bytes 327712 | tf_op jit(solution)/shard_map/ppermute | solution.py:22
  299.4 62.0 %all-gather.12.cloned.1.call-done = bf16[10240,128]{0,1:T(8,128)(2,1)} async-done(((bf16[640,128]{0,1:T(8,128)(2,1)}), bf16[10240,128]{0,1:T(8,128)(2,1)}) %all-gather.12.cloned.1.call-update) | async-done | bytes 2621456 | tf_op jit(solution)/shard_map/all_gather | solution.py:12
  373.7 7.6 collective-permute-done.10
  381.4 4.2 collective-permute-start.11
  385.6 14.2 %collective-permute-done.11 = f32[640,128]{0,1:T(8,128)S(1)} collective-permute-done((f32[640,128]{0,1:T(8,128)S(1)}, f32[640,128]{0,1:T(8,128)S(1)}, u32[]{:S(2)}, u32[]{:S(2)}) %collective-permute-start.11) | collective-permute-done | bytes 327712 | tf_op jit(solution)/shard_map/ppermute | solution.py:22
  399.8 7.4 collective-permute-start.12
  407.2 28.2 %collective-permute-done.12 = f32[640,128]{0,1:T(8,128)S(1)} collective-permute-done((f32[640,128]{0,1:T(8,128)S(1)}, f32[640,128]{0,1:T(8,128)S(1)}, u32[]{:S(2)}, u32[]{:S(2)}) %collective-permute-start.12) | collective-permute-done | bytes 327712 | tf_op jit(solution)/shard_map/ppermute | solution.py:22
  435.4 18.2 %collective-permute-start.13 = (f32[640,128]{0,1:T(8,128)S(1)}, f32[640,128]{0,1:T(8,128)S(1)}, u32[]{:S(2)}, u32[]{:S(2)}) collective-permute-start(f32[640,128]{0,1:T(8,128)S(1)} %add.123), channel_id=1, source_target_pairs={{0,256},{256,0},{16,272},{272,16},{32,288},{288,32},{48,304},{304,... | collective-permute-start | bytes 983048 | tf_op jit(solution)/shard_map/ppermute | solution.py:22
  453.7 14.1 %collective-permute-done.13 = f32[640,128]{0,1:T(8,128)S(1)} collective-permute-done((f32[640,128]{0,1:T(8,128)S(1)}, f32[640,128]{0,1:T(8,128)S(1)}, u32[]{:S(2)}, u32[]{:S(2)}) %collective-permute-start.13) | collective-permute-done | bytes 327712 | tf_op jit(solution)/shard_map/ppermute | solution.py:22
  468.5 58.6 %all-gather.14.cloned.1.call-done = bf16[10240,128]{0,1:T(8,128)(2,1)} async-done(((bf16[640,128]{0,1:T(8,128)(2,1)}), bf16[10240,128]{0,1:T(8,128)(2,1)}) %all-gather.14.cloned.1.call-update) | async-done | bytes 2621456 | tf_op jit(solution)/shard_map/all_gather | solution.py:12
  539.5 7.6 collective-permute-done.15
  551.4 14.2 %collective-permute-done.16 = f32[640,128]{0,1:T(8,128)S(1)} collective-permute-done((f32[640,128]{0,1:T(8,128)S(1)}, f32[640,128]{0,1:T(8,128)S(1)}, u32[]{:S(2)}, u32[]{:S(2)}) %collective-permute-start.16) | collective-permute-done | bytes 327712 | tf_op jit(solution)/shard_map/ppermute | solution.py:22
  565.6 7.4 collective-permute-start.17
  573.0 28.2 %collective-permute-done.17 = f32[640,128]{0,1:T(8,128)S(1)} collective-permute-done((f32[640,128]{0,1:T(8,128)S(1)}, f32[640,128]{0,1:T(8,128)S(1)}, u32[]{:S(2)}, u32[]{:S(2)}) %collective-permute-start.17) | collective-permute-done | bytes 327712 | tf_op jit(solution)/shard_map/ppermute | solution.py:22
  601.2 18.2 %collective-permute-start.18 = (f32[640,128]{0,1:T(8,128)S(1)}, f32[640,128]{0,1:T(8,128)S(1)}, u32[]{:S(2)}, u32[]{:S(2)}) collective-permute-start(f32[640,128]{0,1:T(8,128)S(1)} %add.128), channel_id=1, source_target_pairs={{0,256},{256,0},{16,272},{272,16},{32,288},{288,32},{48,304},{304,... | collective-permute-start | bytes 983048 | tf_op jit(solution)/shard_map/ppermute | solution.py:22
  619.5 14.1 %collective-permute-done.18 = f32[640,128]{0,1:T(8,128)S(1)} collective-permute-done((f32[640,128]{0,1:T(8,128)S(1)}, f32[640,128]{0,1:T(8,128)S(1)}, u32[]{:S(2)}, u32[]{:S(2)}) %collective-permute-start.18) | collective-permute-done | bytes 327712 | tf_op jit(solution)/shard_map/ppermute | solution.py:22
  634.6 69.9 %all-gather.8.cloned.1.call-done = bf16[16,640,256]{2,1,0:T(8,128)(2,1)} async-done(((bf16[1,640,256]{2,1,0:T(8,128)(2,1)}), bf16[16,640,256]{2,1,0:T(8,128)(2,1)}) %all-gather.8.cloned.1.call-update) | async-done | bytes 5242896 | tf_op jit(solution)/shard_map/all_gather | solution.py:12
  715.7 7.6 collective-permute-done.20
  723.3 4.2 collective-permute-start.21
  727.5 14.2 %collective-permute-done.21 = f32[640,128]{0,1:T(8,128)S(1)} collective-permute-done((f32[640,128]{0,1:T(8,128)S(1)}, f32[640,128]{0,1:T(8,128)S(1)}, u32[]{:S(2)}, u32[]{:S(2)}) %collective-permute-start.21) | collective-permute-done | bytes 327712 | tf_op jit(solution)/shard_map/ppermute | solution.py:22
  741.7 7.4 collective-permute-start.22
  749.1 28.2 %collective-permute-done.22 = f32[640,128]{0,1:T(8,128)S(1)} collective-permute-done((f32[640,128]{0,1:T(8,128)S(1)}, f32[640,128]{0,1:T(8,128)S(1)}, u32[]{:S(2)}, u32[]{:S(2)}) %collective-permute-start.22) | collective-permute-done | bytes 327712 | tf_op jit(solution)/shard_map/ppermute | solution.py:22
  (84 shorter events, 73.9 us)
Async XLA Ops:
  6.5 139.9 %copy-start = (bf16[1,640,640]{2,1,0:T(8,128)(2,1)S(1)}, bf16[1,640,640]{2,1,0:T(8,128)(2,1)}, u32[]{:S(2)}) copy-start(bf16[1,640,640]{2,1,0:T(8,128)(2,1)} %param.9) | copy-start | bytes 2457604
  6.5 45.1 %copy-start.4 = (s32[2,32]{1,0:T(2,128)S(1)}, s32[2,32]{1,0:T(2,128)}, u32[]{:S(2)}) copy-start(s32[2,32]{1,0:T(2,128)} %param.7) | copy-start | bytes 772
  6.5 136.4 %all-gather.10.cloned.1.call-start = ((), (), s32[]{:S(2)}) async-start(), calls=%async_computation.1 | async-start | bytes 2785280 | tf_op jit(solution)/shard_map/all_gather | solution.py:12
  7.7 10.0 %collective-permute-start = (f32[640,128]{0,1:T(8,128)S(1)}, f32[640,128]{0,1:T(8,128)S(1)}, u32[]{:S(2)}, u32[]{:S(2)}) collective-permute-start(f32[640,128]{0,1:T(8,128)S(1)} %bitcast_convert_fusion), channel_id=1, source_target_pairs={{0,16},{16,0},{32,48},{48,32},{64,80},{80,64},{96,112},{112,96},{1... | collective-permute-start | bytes 983048 | tf_op jit(solution)/shard_map/ppermute | solution.py:22
  17.8 10.8 %collective-permute-start.1 = (f32[640,128]{0,1:T(8,128)S(1)}, f32[640,128]{0,1:T(8,128)S(1)}, u32[]{:S(2)}, u32[]{:S(2)}) collective-permute-start(f32[640,128]{0,1:T(8,128)S(1)} %fusion.24), channel_id=1, source_target_pairs={{0,32},{32,0},{16,48},{48,16},{64,96},{96,64},{80,112},{112,80},{1... | collective-permute-start | bytes 983048 | tf_op jit(solution)/shard_map/ppermute | solution.py:22
  28.6 19.4 %collective-permute-start.2 = (f32[640,128]{0,1:T(8,128)S(1)}, f32[640,128]{0,1:T(8,128)S(1)}, u32[]{:S(2)}, u32[]{:S(2)}) collective-permute-start(f32[640,128]{0,1:T(8,128)S(1)} %add.109), channel_id=1, source_target_pairs={{0,64},{64,0},{16,80},{80,16},{32,96},{96,32},{48,112},{112,48},{1... | collective-permute-start | bytes 983048 | tf_op jit(solution)/shard_map/ppermute | solution.py:22
  48.1 33.9 %collective-permute-start.3 = (f32[640,128]{0,1:T(8,128)S(1)}, f32[640,128]{0,1:T(8,128)S(1)}, u32[]{:S(2)}, u32[]{:S(2)}) collective-permute-start(f32[640,128]{0,1:T(8,128)S(1)} %add.110), channel_id=1, source_target_pairs={{0,128},{128,0},{16,144},{144,16},{32,160},{160,32},{48,176},{176,... | collective-permute-start | bytes 983048 | tf_op jit(solution)/shard_map/ppermute | solution.py:22
  82.7 278.6 %all-gather.12.cloned.1.call-start = ((), (), s32[]{:S(2)}) async-start(), calls=%async_computation.2 | async-start | bytes 2785280 | tf_op jit(solution)/shard_map/all_gather | solution.py:12
  145.2 1.7 copy-start.1
  147.2 5.8 collective-permute-start.4
  153.1 17.8 %collective-permute-start.5 = (f32[1280,128]{0,1:T(8,128)S(1)}, f32[1280,128]{0,1:T(8,128)S(1)}, u32[]{:S(2)}, u32[]{:S(2)}) collective-permute-start(f32[1280,128]{0,1:T(8,128)S(1)} %fusion.31), channel_id=1, source_target_pairs={{0,32},{32,0},{16,48},{48,16},{64,96},{96,64},{80,112},{112,80},{1... | collective-permute-start | bytes 1966088 | tf_op jit(solution)/shard_map/ppermute | solution.py:22
  171.0 32.4 %collective-permute-start.6 = (f32[1280,128]{0,1:T(8,128)S(1)}, f32[1280,128]{0,1:T(8,128)S(1)}, u32[]{:S(2)}, u32[]{:S(2)}) collective-permute-start(f32[1280,128]{0,1:T(8,128)S(1)} %add.113), channel_id=1, source_target_pairs={{0,64},{64,0},{16,80},{80,16},{32,96},{96,32},{48,112},{112,48},{1... | collective-permute-start | bytes 1966088 | tf_op jit(solution)/shard_map/ppermute | solution.py:22
  203.5 70.8 %collective-permute-start.7 = (f32[1280,128]{0,1:T(8,128)S(1)}, f32[1280,128]{0,1:T(8,128)S(1)}, u32[]{:S(2)}, u32[]{:S(2)}) collective-permute-start(f32[1280,128]{0,1:T(8,128)S(1)} %add.114), channel_id=1, source_target_pairs={{0,128},{128,0},{16,144},{144,16},{32,160},{160,32},{48,176},{176,... | collective-permute-start | bytes 1966088 | tf_op jit(solution)/shard_map/ppermute | solution.py:22
  274.4 24.2 %collective-permute-start.8 = (f32[640,128]{0,1:T(8,128)S(1)}, f32[640,128]{0,1:T(8,128)S(1)}, u32[]{:S(2)}, u32[]{:S(2)}) collective-permute-start(f32[640,128]{0,1:T(8,128)S(1)} %get-tuple-element.6), channel_id=1, source_target_pairs={{0,256},{256,0},{16,272},{272,16},{32,288},{288,32},{48,304},{304,... | collective-permute-start | bytes 983048 | tf_op jit(solution)/shard_map/ppermute | solution.py:22
  299.3 227.8 %all-gather.14.cloned.1.call-start = ((), (), s32[]{:S(2)}) async-start(), calls=%async_computation.3 | async-start | bytes 2785280 | tf_op jit(solution)/shard_map/all_gather | solution.py:12
  365.2 5.3 collective-permute-start.9
  370.5 10.8 %collective-permute-start.10 = (f32[640,128]{0,1:T(8,128)S(1)}, f32[640,128]{0,1:T(8,128)S(1)}, u32[]{:S(2)}, u32[]{:S(2)}) collective-permute-start(f32[640,128]{0,1:T(8,128)S(1)} %add.120), channel_id=1, source_target_pairs={{0,32},{32,0},{16,48},{48,16},{64,96},{96,64},{80,112},{112,80},{1... | collective-permute-start | bytes 983048 | tf_op jit(solution)/shard_map/ppermute | solution.py:22
  381.4 18.4 %collective-permute-start.11 = (f32[640,128]{0,1:T(8,128)S(1)}, f32[640,128]{0,1:T(8,128)S(1)}, u32[]{:S(2)}, u32[]{:S(2)}) collective-permute-start(f32[640,128]{0,1:T(8,128)S(1)} %add.121), channel_id=1, source_target_pairs={{0,64},{64,0},{16,80},{80,16},{32,96},{96,32},{48,112},{112,48},{1... | collective-permute-start | bytes 983048 | tf_op jit(solution)/shard_map/ppermute | solution.py:22
  399.8 35.6 %collective-permute-start.12 = (f32[640,128]{0,1:T(8,128)S(1)}, f32[640,128]{0,1:T(8,128)S(1)}, u32[]{:S(2)}, u32[]{:S(2)}) collective-permute-start(f32[640,128]{0,1:T(8,128)S(1)} %add.122), channel_id=1, source_target_pairs={{0,128},{128,0},{16,144},{144,16},{32,160},{160,32},{48,176},{176,... | collective-permute-start | bytes 983048 | tf_op jit(solution)/shard_map/ppermute | solution.py:22
  435.4 32.3 %collective-permute-start.13 = (f32[640,128]{0,1:T(8,128)S(1)}, f32[640,128]{0,1:T(8,128)S(1)}, u32[]{:S(2)}, u32[]{:S(2)}) collective-permute-start(f32[640,128]{0,1:T(8,128)S(1)} %add.123), channel_id=1, source_target_pairs={{0,256},{256,0},{16,272},{272,16},{32,288},{288,32},{48,304},{304,... | collective-permute-start | bytes 983048 | tf_op jit(solution)/shard_map/ppermute | solution.py:22
  468.5 236.0 %all-gather.8.cloned.1.call-start = ((), (), s32[]{:S(2)}) async-start(), calls=%async_computation | async-start | bytes 5570560 | tf_op jit(solution)/shard_map/all_gather | solution.py:12
  529.4 1.3 copy-start.2
  531.0 5.3 collective-permute-start.14
  536.3 10.8 %collective-permute-start.15 = (f32[640,128]{0,1:T(8,128)S(1)}, f32[640,128]{0,1:T(8,128)S(1)}, u32[]{:S(2)}, u32[]{:S(2)}) collective-permute-start(f32[640,128]{0,1:T(8,128)S(1)} %add.125), channel_id=1, source_target_pairs={{0,32},{32,0},{16,48},{48,16},{64,96},{96,64},{80,112},{112,80},{1... | collective-permute-start | bytes 983048 | tf_op jit(solution)/shard_map/ppermute | solution.py:22
  547.2 18.4 %collective-permute-start.16 = (f32[640,128]{0,1:T(8,128)S(1)}, f32[640,128]{0,1:T(8,128)S(1)}, u32[]{:S(2)}, u32[]{:S(2)}) collective-permute-start(f32[640,128]{0,1:T(8,128)S(1)} %add.126), channel_id=1, source_target_pairs={{0,64},{64,0},{16,80},{80,16},{32,96},{96,32},{48,112},{112,48},{1... | collective-permute-start | bytes 983048 | tf_op jit(solution)/shard_map/ppermute | solution.py:22
  565.6 35.6 %collective-permute-start.17 = (f32[640,128]{0,1:T(8,128)S(1)}, f32[640,128]{0,1:T(8,128)S(1)}, u32[]{:S(2)}, u32[]{:S(2)}) collective-permute-start(f32[640,128]{0,1:T(8,128)S(1)} %add.127), channel_id=1, source_target_pairs={{0,128},{128,0},{16,144},{144,16},{32,160},{160,32},{48,176},{176,... | collective-permute-start | bytes 983048 | tf_op jit(solution)/shard_map/ppermute | solution.py:22
  601.2 32.3 %collective-permute-start.18 = (f32[640,128]{0,1:T(8,128)S(1)}, f32[640,128]{0,1:T(8,128)S(1)}, u32[]{:S(2)}, u32[]{:S(2)}) collective-permute-start(f32[640,128]{0,1:T(8,128)S(1)} %add.128), channel_id=1, source_target_pairs={{0,256},{256,0},{16,272},{272,16},{32,288},{288,32},{48,304},{304,... | collective-permute-start | bytes 983048 | tf_op jit(solution)/shard_map/ppermute | solution.py:22
  634.6 73.6 %copy-start.3 = (bf16[1,640,640]{2,1,0:T(8,128)(2,1)S(1)}, bf16[1,640,640]{2,1,0:T(8,128)(2,1)}, u32[]{:S(2)}) copy-start(bf16[1,640,640]{2,1,0:T(8,128)(2,1)} %param.11) | copy-start | bytes 2457604
  708.6 3.8 collective-permute-start.19
  712.5 10.8 %collective-permute-start.20 = (f32[640,128]{0,1:T(8,128)S(1)}, f32[640,128]{0,1:T(8,128)S(1)}, u32[]{:S(2)}, u32[]{:S(2)}) collective-permute-start(f32[640,128]{0,1:T(8,128)S(1)} %add.130), channel_id=1, source_target_pairs={{0,32},{32,0},{16,48},{48,16},{64,96},{96,64},{80,112},{112,80},{1... | collective-permute-start | bytes 983048 | tf_op jit(solution)/shard_map/ppermute | solution.py:22
  723.3 18.4 %collective-permute-start.21 = (f32[640,128]{0,1:T(8,128)S(1)}, f32[640,128]{0,1:T(8,128)S(1)}, u32[]{:S(2)}, u32[]{:S(2)}) collective-permute-start(f32[640,128]{0,1:T(8,128)S(1)} %add.131), channel_id=1, source_target_pairs={{0,64},{64,0},{16,80},{80,16},{32,96},{96,32},{48,112},{112,48},{1... | collective-permute-start | bytes 983048 | tf_op jit(solution)/shard_map/ppermute | solution.py:22
  741.7 35.6 %collective-permute-start.22 = (f32[640,128]{0,1:T(8,128)S(1)}, f32[640,128]{0,1:T(8,128)S(1)}, u32[]{:S(2)}, u32[]{:S(2)}) collective-permute-start(f32[640,128]{0,1:T(8,128)S(1)} %add.132), channel_id=1, source_target_pairs={{0,128},{128,0},{16,144},{144,16},{32,160},{160,32},{48,176},{176,... | collective-permute-start | bytes 983048 | tf_op jit(solution)/shard_map/ppermute | solution.py:22
Sparse Core Ops, SparseCore 0:
  82.8 60.0 all-gather.9
  299.4 61.8 all-gather.11
  468.6 58.4 all-gather.13
  634.7 69.7 all-gather.7
